TPU v7x, 256 devices: a whole 4x4x8 slice. The times are simulated.
256 devices in a mesh: seq: 32 (over x, z), ch: 8 (over y, core).
Axes of the slice: x: 4, y: 4, z: 8, core: 2. Of those that a mesh axis runs over, the one named last changes fastest.
Arguments:
- out_gate: bfloat16 [12288, 4096], P('seq', 'ch'), may hold values from -6 to 6
- in_gate: bfloat16 [12288, 4096], P('seq', 'ch'), may hold values from -6 to 6
- values: bfloat16 [12288, 4096], P('seq', 'ch'), may hold values from -6 to 6
- short_filter: float32 [3, 3, 4096], P(None, None, 'ch'), may hold values from -3 to 3
- long_filter: float32 [12288, 4096], P('seq', 'ch'), may hold values from -1.5 to 1.5
- skip_gain: float32 [4096], P('ch'), may hold values from -4 to 4
- out_weight: bfloat16 [4096, 4096], P(None, 'ch'), may hold values from -0.09375 to 0.09375
Outputs:
- projected: bfloat16 [12288, 4096], P('seq', 'ch')
All inputs are finite; a program needn't handle non-finite values.
Results may differ from a plain program's by a relative error of at most 0.0049.
Values may be sent and summed in bfloat16 or wider, within the bound.
A program may use at most 128 MiB of HBM per device.

v0:
```python
import math
import jax
import jax.numpy as jnp
from jax import lax
from jax.sharding import PartitionSpec as P

highest = lax.Precision.HIGHEST


def shifted(block, axis, distance):
    devices = range(lax.axis_size(axis))
    route = [(i - distance, i) for i in devices if i - distance in devices]
    return lax.ppermute(block, axis, route)


def phase_table(row_ids, col_ids, modulus, direction):
    product = row_ids[:, None] * col_ids[None, :] % modulus
    angles = product.astype(jnp.float32) * (direction * 2.0 * math.pi / modulus)
    return (jnp.cos(angles), jnp.sin(angles))


def contract(pattern, first_op, second_op):
    return jnp.einsum(pattern, first_op, second_op, precision=highest)


def complex_apply(pattern, phases, operand):
    cosine, sine_part = phases
    real_part, imaginary = operand
    return (
        contract(pattern, cosine, real_part) - contract(pattern, sine_part, imaginary),
        contract(pattern, cosine, imaginary) + contract(pattern, sine_part, real_part),
    )


def complex_times(first_op, second_op):
    return (
        first_op[0] * second_op[0] - first_op[1] * second_op[1],
        first_op[0] * second_op[1] + first_op[1] * second_op[0],
    )


def sequence_conv(mixed_in, long_filter):
    seq_count = lax.axis_size("seq")
    seq_index = lax.axis_index("seq")
    row_count = mixed_in.shape[0]
    total_len = row_count * seq_count
    piece_rows = row_count // seq_count
    rows_b = jnp.arange(row_count, dtype=jnp.int32)
    device_ids = jnp.arange(seq_count, dtype=jnp.int32)
    positions = seq_index * row_count + rows_b
    angles = positions.astype(jnp.float32) * (math.pi / total_len)
    cosines = jnp.cos(angles)[:, None]
    sines = jnp.sin(angles)[:, None]
    planes = jnp.stack([mixed_in, long_filter])[:, None]
    spread = lax.all_to_all(planes, "seq", split_axis=2, concat_axis=1, tiled=True)
    local_b = seq_index * piece_rows + jnp.arange(piece_rows, dtype=jnp.int32)
    arrived_pos = device_ids[:, None] * row_count + local_b[None, :]
    arrived_angles = arrived_pos.astype(jnp.float32) * (math.pi / total_len)
    arrived_cos = jnp.cos(arrived_angles)[:, :, None]
    arrived_sin = jnp.sin(arrived_angles)[:, :, None]
    zeros_plane = jnp.zeros_like(spread[0])
    real_part = jnp.stack([spread[0], spread[0] * arrived_cos, spread[1], spread[1] * arrived_cos])
    imaginary = jnp.stack(
        [zeros_plane, -spread[0] * arrived_sin, zeros_plane, -spread[1] * arrived_sin]
    )
    sectioned = complex_apply(
        "kp,xpbc->xkbc",
        phase_table(device_ids, device_ids, seq_count, -1.0),
        (real_part, imaginary),
    )
    twist_table = phase_table(device_ids, local_b, total_len, -1.0)
    sectioned = complex_times(sectioned, (twist_table[0][:, :, None], twist_table[1][:, :, None]))
    arrived = (
        lax.all_to_all(sectioned[0], "seq", split_axis=1, concat_axis=2, tiled=True),
        lax.all_to_all(sectioned[1], "seq", split_axis=1, concat_axis=2, tiled=True),
    )
    spectra = complex_apply("mb,xkbc->xkmc", phase_table(rows_b, rows_b, row_count, -1.0), arrived)
    product = complex_times((spectra[0][:2], spectra[1][:2]), (spectra[0][2:], spectra[1][2:]))
    sectioned = complex_apply("mb,xkmc->xkbc", phase_table(rows_b, rows_b, row_count, 1.0), product)
    twist_table = phase_table(seq_index.reshape(1), rows_b, total_len, 1.0)
    sectioned = complex_times(sectioned, (twist_table[0][:, :, None], twist_table[1][:, :, None]))
    returned = (
        lax.all_to_all(sectioned[0], "seq", split_axis=2, concat_axis=1, tiled=True),
        lax.all_to_all(sectioned[1], "seq", split_axis=2, concat_axis=1, tiled=True),
    )
    sectioned = complex_apply(
        "kp,xkbc->xpbc", phase_table(device_ids, device_ids, seq_count, 1.0), returned
    )
    restored = (
        lax.all_to_all(sectioned[0], "seq", split_axis=1, concat_axis=2, tiled=True),
        lax.all_to_all(sectioned[1], "seq", split_axis=1, concat_axis=2, tiled=True),
    )
    real_out = restored[0][:, 0] / total_len
    imag_out = restored[1][:, 0] / total_len
    return 0.5 * (real_out[0] + cosines * real_out[1] - sines * imag_out[1])


def on_device(out_gate, in_gate, values, short_filter, long_filter, skip_gain, out_weight):
    tap_count = short_filter.shape[1]
    row_count = out_gate.shape[0]
    stacked = jnp.stack([out_gate, in_gate, values])
    rim_rows = shifted(stacked[:, row_count - (tap_count - 1) :], "seq", 1)
    widened = jnp.concatenate([rim_rows, stacked], axis=1).astype(jnp.float32)
    shorted = short_filter[:, 0, None, :] * widened[:, tap_count - 1 :]
    for offset in range(1, tap_count):
        start_row = tap_count - 1 - offset
        shorted = (
            shorted
            + short_filter[:, offset, None, :] * widened[:, start_row : start_row + row_count]
        )
    gate_late = shorted[0]
    mixed_in = shorted[1] * shorted[2]
    long_out = sequence_conv(mixed_in, long_filter)
    filtered = long_out + skip_gain * mixed_in
    mixed = (gate_late * filtered).astype(jnp.bfloat16)
    summed = jnp.dot(
        lax.all_gather(mixed, "ch", axis=1, tiled=True),
        out_weight,
        preferred_element_type=jnp.float32,
    )
    return summed.astype(jnp.bfloat16)


def solution(mesh):
    return jax.shard_map(
        on_device,
        mesh=mesh,
        in_specs=(
            P("seq", "ch"),
            P("seq", "ch"),
            P("seq", "ch"),
            P(None, None, "ch"),
            P("seq", "ch"),
            P("ch"),
            P(None, "ch"),
        ),
        out_specs=P("seq", "ch"),
        check_vma=False,
    )
```

profile of v0, /device:TPU:1, one launch (start us, length us, event | category | flops | bytes accessed | tf_op | source)
XLA Modules:
  0.0 544.4 jit_solution(16303291833496536461)
XLA Ops:
  19.1 12.4 %all-to-all-start = ((f32[2,1,384,512]{3,0,1,2:T(2,128)}), f32[2,1,384,512]{3,0,1,2:T(2,128)S(1)}, u32[]{:S(2)}, u32[]{:S(2)}) async-start(f32[2,1,384,512]{3,0,1,2:T(2,128)} %copy.68), calls=%async_computation | async-start | bytes 3145728 | tf_op jit(solution)/shard_map/all_to_all | solution.py:55
  31.7 36.7 %all-to-all-done = f32[2,1,384,512]{3,0,1,2:T(2,128)S(1)} async-done(((f32[2,1,384,512]{3,0,1,2:T(2,128)}), f32[2,1,384,512]{3,0,1,2:T(2,128)S(1)}, u32[]{:S(2)}, u32[]{:S(2)}) %all-to-all-start) | async-done | bytes 1572896 | tf_op jit(solution)/shard_map/all_to_all | solution.py:55
  80.6 6.0 %fusion = (f32[4,32,12,512]{3,1,2,0:T(8,128)S(1)}, f32[4,32,12,512]{3,1,2,0:T(8,128)}) fusion(f32[4,12,512,32]{2,3,1,0:T(8,128)S(1)} %convolution_subtract_fusion, f32[32,12]{0,1:T(8,128)S(1)} %get-tuple-element.27, f32[32,12]{0,1:T(8,128)S(1)} %get-tuple-element.26, f32[4,12,512,32]{2,3,1,0:T(8,128)S(1)} %fusion.2, ...), kind=kOutput, calls=%fused_computation.4 | convolution fusion | flops 309868544 | bytes 15731712 | tf_op jit(solution)/shard_map/kp,xpbc->xkbc/dot_general | solution.py:23
  90.3 7.3 %all-to-all-start.1 = ((f32[4,32,12,512]{3,0,2,1:T(4,128)}), f32[4,32,12,512]{3,0,2,1:T(4,128)S(1)}, u32[]{:S(2)}, u32[]{:S(2)}) async-start(f32[4,32,12,512]{3,0,2,1:T(4,128)} %copy.79), calls=%async_computation.1 | async-start | bytes 6291456 | tf_op jit(solution)/shard_map/all_to_all | solution.py:74
  97.6 5.5 %copy.81 = f32[4,32,12,512]{3,0,2,1:T(4,128)} copy(f32[4,32,12,512]{3,1,2,0:T(8,128)} %get-tuple-element.8) | data formatting | bytes 6291456 | tf_op jit(solution)/shard_map/add | solution.py:38
  103.1 65.8 %all-to-all-done.1 = f32[4,32,12,512]{3,0,2,1:T(4,128)S(1)} async-done(((f32[4,32,12,512]{3,0,2,1:T(4,128)}), f32[4,32,12,512]{3,0,2,1:T(4,128)S(1)}, u32[]{:S(2)}, u32[]{:S(2)}) %all-to-all-start.1) | async-done | bytes 3145760 | tf_op jit(solution)/shard_map/all_to_all | solution.py:74
  170.6 7.8 %all-to-all-start.2 = ((f32[4,32,12,512]{3,0,2,1:T(4,128)}), f32[4,32,12,512]{3,0,2,1:T(4,128)}, u32[]{:S(2)}, u32[]{:S(2)}) async-start(f32[4,32,12,512]{3,0,2,1:T(4,128)} %copy.81), calls=%async_computation.2 | async-start | bytes 6291456 | tf_op jit(solution)/shard_map/all_to_all | solution.py:75
  181.7 9.8 %fusion.43 = f32[4,512,384]{2,1,0:T(8,128)} fusion(f32[4,384,512]{1,2,0:T(8,128)S(1)} %copy.80), kind=kOutput, calls=%fused_computation.73 | convolution fusion | flops 3625205760 | bytes 6291456 | tf_op jit(solution)/shard_map/mb,xkbc->xkmc/dot_general | solution.py:23
  191.5 60.2 %all-to-all-done.2 = f32[4,32,12,512]{3,0,2,1:T(4,128)} async-done(((f32[4,32,12,512]{3,0,2,1:T(4,128)}), f32[4,32,12,512]{3,0,2,1:T(4,128)}, u32[]{:S(2)}, u32[]{:S(2)}) %all-to-all-start.2) | async-done | bytes 3145760 | tf_op jit(solution)/shard_map/all_to_all | solution.py:75
  256.8 10.7 %fusion.41 = f32[4,512,384]{2,1,0:T(8,128)S(1)} fusion(f32[4,384,512]{1,2,0:T(8,128)} %copy.82), kind=kOutput, calls=%fused_computation.71 | convolution fusion | flops 3625205760 | bytes 6291456 | tf_op jit(solution)/shard_map/mb,xkbc->xkmc/dot_general | solution.py:23
  267.6 9.2 %subtract_bitcast_fusion = f32[4,1,384,512]{2,3,0,1:T(8,128)S(1)} fusion(f32[4,512,384]{2,1,0:T(8,128)S(1)} %copy-done.4, f32[4,384,512]{1,2,0:T(8,128)S(1)} %copy-done), kind=kOutput, calls=%fused_computation.9 | convolution fusion | flops 3625992192 | bytes 9437184 | tf_op jit(solution)/shard_map/mb,xkbc->xkmc/dot_general | solution.py:23
  276.8 9.0 %add_bitcast_fusion = f32[4,1,384,512]{2,3,0,1:T(8,128)S(1)} fusion(f32[4,512,384]{2,1,0:T(8,128)S(1)} %fusion.41, f32[4,384,512]{1,2,0:T(8,128)S(1)} %copy.80), kind=kOutput, calls=%fused_computation.8 | convolution fusion | flops 3625992192 | bytes 9437184 | tf_op jit(solution)/shard_map/mb,xkbc->xkmc/dot_general | solution.py:23
  291.5 5.8 %fusion.10 = f32[2,512,384]{2,1,0:T(8,128)S(1)} fusion(f32[2,1,384,512]{2,3,0,1:T(8,128)S(1)} %get-tuple-element.10), kind=kOutput, calls=%fused_computation.28 | convolution fusion | flops 1813266432 | bytes 3145728 | tf_op jit(solution)/shard_map/mb,xkmc->xkbc/dot_general | solution.py:23
  302.8 5.5 %fusion.7 = (f32[2,1,384,512]{2,3,0,1:T(8,128)S(1)}, f32[2,1,384,512]{2,3,0,1:T(8,128)S(1)}) fusion(f32[2,512,384]{2,1,0:T(8,128)S(1)} %fusion.18, f32[384]{0:T(512)S(1)} %get-tuple-element.32, f32[384]{0:T(512)S(1)} %get-tuple-element.33, f32[2,512,384]{2,1,0:T(8,128)S(1)} %fusion.10, f32[2,1,384,512]{2,3,0,1:T(8,128)S(1)} %get-tuple-element.9), kind=kOutput, calls=%fused_computation.23 | convolution fusion | flops 1816018944 | bytes 7867392 | tf_op jit(solution)/shard_map/mb,xkmc->xkbc/dot_general | solution.py:23
  310.4 5.9 %all-to-all-start.3 = ((f32[2,1,384,512]{3,0,1,2:T(2,128)}), f32[2,1,384,512]{3,0,1,2:T(2,128)S(1)}, u32[]{:S(2)}, u32[]{:S(2)}) async-start(f32[2,1,384,512]{3,0,1,2:T(2,128)} %copy.85), calls=%async_computation.3 | async-start | bytes 3145728 | tf_op jit(solution)/shard_map/all_to_all | solution.py:83
  318.3 34.6 %all-to-all-done.3 = f32[2,1,384,512]{3,0,1,2:T(2,128)S(1)} async-done(((f32[2,1,384,512]{3,0,1,2:T(2,128)}), f32[2,1,384,512]{3,0,1,2:T(2,128)S(1)}, u32[]{:S(2)}, u32[]{:S(2)}) %all-to-all-start.3) | async-done | bytes 1572896 | tf_op jit(solution)/shard_map/all_to_all | solution.py:83
  352.9 7.7 %all-to-all-start.4 = ((f32[2,1,384,512]{3,0,1,2:T(2,128)}), f32[2,1,384,512]{3,0,1,2:T(2,128)S(1)}, u32[]{:S(2)}, u32[]{:S(2)}) async-start(f32[2,1,384,512]{3,0,1,2:T(2,128)} %copy.87), calls=%async_computation.4 | async-start | bytes 3145728 | tf_op jit(solution)/shard_map/all_to_all | solution.py:84
  364.3 33.1 %all-to-all-done.4 = f32[2,1,384,512]{3,0,1,2:T(2,128)S(1)} async-done(((f32[2,1,384,512]{3,0,1,2:T(2,128)}), f32[2,1,384,512]{3,0,1,2:T(2,128)S(1)}, u32[]{:S(2)}, u32[]{:S(2)}) %all-to-all-start.4) | async-done | bytes 1572896 | tf_op jit(solution)/shard_map/all_to_all | solution.py:84
  403.9 7.8 %all-to-all-start.5 = ((f32[2,32,12,512]{3,0,2,1:T(2,128)}), f32[2,32,12,512]{3,0,2,1:T(2,128)}, u32[]{:S(2)}, u32[]{:S(2)}) async-start(f32[2,32,12,512]{3,0,2,1:T(2,128)} %copy.89), calls=%async_computation.5 | async-start | bytes 3145728 | tf_op jit(solution)/shard_map/all_to_all | solution.py:90
  419.2 29.2 %all-to-all-done.5 = f32[2,32,12,512]{3,0,2,1:T(2,128)} async-done(((f32[2,32,12,512]{3,0,2,1:T(2,128)}), f32[2,32,12,512]{3,0,2,1:T(2,128)}, u32[]{:S(2)}, u32[]{:S(2)}) %all-to-all-start.5) | async-done | bytes 1572896 | tf_op jit(solution)/shard_map/all_to_all | solution.py:90
  448.4 7.8 %all-to-all-start.6 = ((f32[2,32,12,512]{3,0,2,1:T(2,128)}), f32[2,32,12,512]{3,0,2,1:T(2,128)}, u32[]{:S(2)}, u32[]{:S(2)}) async-start(f32[2,32,12,512]{3,0,2,1:T(2,128)} %copy.92), calls=%async_computation.6 | async-start | bytes 3145728 | tf_op jit(solution)/shard_map/all_to_all | solution.py:91
  464.9 28.1 %all-to-all-done.6 = f32[2,32,12,512]{3,0,2,1:T(2,128)} async-done(((f32[2,32,12,512]{3,0,2,1:T(2,128)}), f32[2,32,12,512]{3,0,2,1:T(2,128)}, u32[]{:S(2)}, u32[]{:S(2)}) %all-to-all-start.6) | async-done | bytes 1572896 | tf_op jit(solution)/shard_map/all_to_all | solution.py:91
  500.7 31.0 %all-gather.2.cloned.1.call-done = bf16[384,4096]{1,0:T(8,128)(2,1)} async-done(((bf16[384,512]{1,0:T(8,128)(2,1)}), bf16[384,4096]{1,0:T(8,128)(2,1)}) %all-gather.2.cloned.1.call-update) | async-done | bytes 3145744 | tf_op jit(solution)/shard_map/all_gather | solution.py:117
  531.6 5.7 %convolution_convert_fusion = bf16[384,512]{1,0:T(8,128)(2,1)} fusion(bf16[384,4096]{1,0:T(8,128)(2,1)} %all-gather.2.cloned.1.call-done, bf16[4096,512]{1,0:T(8,128)(2,1)} %param.13), kind=kOutput, calls=%fused_computation.48 | convolution fusion | flops 1610809344 | bytes 7733248 | tf_op jit(solution)/shard_map/dot_general | solution.py:116
  (60 shorter events, 87.9 us)
Async XLA Ops:
  7.3 5.3 collective-permute-start
  14.9 1.8 copy-start.1
  14.9 1.7 copy-start.5
  19.1 49.3 %all-to-all-start = ((f32[2,1,384,512]{3,0,1,2:T(2,128)}), f32[2,1,384,512]{3,0,1,2:T(2,128)S(1)}, u32[]{:S(2)}, u32[]{:S(2)}) async-start(f32[2,1,384,512]{3,0,1,2:T(2,128)} %copy.68), calls=%async_computation | async-start | bytes 3145728 | tf_op jit(solution)/shard_map/all_to_all | solution.py:55
  90.3 78.6 %all-to-all-start.1 = ((f32[4,32,12,512]{3,0,2,1:T(4,128)}), f32[4,32,12,512]{3,0,2,1:T(4,128)S(1)}, u32[]{:S(2)}, u32[]{:S(2)}) async-start(f32[4,32,12,512]{3,0,2,1:T(4,128)} %copy.79), calls=%async_computation.1 | async-start | bytes 6291456 | tf_op jit(solution)/shard_map/all_to_all | solution.py:74
  168.9 1.7 copy-start.3
  170.6 81.0 %all-to-all-start.2 = ((f32[4,32,12,512]{3,0,2,1:T(4,128)}), f32[4,32,12,512]{3,0,2,1:T(4,128)}, u32[]{:S(2)}, u32[]{:S(2)}) async-start(f32[4,32,12,512]{3,0,2,1:T(4,128)} %copy.81), calls=%async_computation.2 | async-start | bytes 6291456 | tf_op jit(solution)/shard_map/all_to_all | solution.py:75
  256.8 10.7 %copy-start = (f32[4,384,512]{1,2,0:T(8,128)S(1)}, f32[4,384,512]{1,2,0:T(8,128)}, u32[]{:S(2)}) copy-start(f32[4,384,512]{1,2,0:T(8,128)} %copy.82) | copy-start | bytes 9437188
  256.8 10.7 %copy-start.4 = (f32[4,512,384]{2,1,0:T(8,128)S(1)}, f32[4,512,384]{2,1,0:T(8,128)}, u32[]{:S(2)}) copy-start(f32[4,512,384]{2,1,0:T(8,128)} %fusion.43) | copy-start | bytes 9437188
  310.4 42.6 %all-to-all-start.3 = ((f32[2,1,384,512]{3,0,1,2:T(2,128)}), f32[2,1,384,512]{3,0,1,2:T(2,128)S(1)}, u32[]{:S(2)}, u32[]{:S(2)}) async-start(f32[2,1,384,512]{3,0,1,2:T(2,128)} %copy.85), calls=%async_computation.3 | async-start | bytes 3145728 | tf_op jit(solution)/shard_map/all_to_all | solution.py:83
  352.9 44.5 %all-to-all-start.4 = ((f32[2,1,384,512]{3,0,1,2:T(2,128)}), f32[2,1,384,512]{3,0,1,2:T(2,128)S(1)}, u32[]{:S(2)}, u32[]{:S(2)}) async-start(f32[2,1,384,512]{3,0,1,2:T(2,128)} %copy.87), calls=%async_computation.4 | async-start | bytes 3145728 | tf_op jit(solution)/shard_map/all_to_all | solution.py:84
  403.9 44.6 %all-to-all-start.5 = ((f32[2,32,12,512]{3,0,2,1:T(2,128)}), f32[2,32,12,512]{3,0,2,1:T(2,128)}, u32[]{:S(2)}, u32[]{:S(2)}) async-start(f32[2,32,12,512]{3,0,2,1:T(2,128)} %copy.89), calls=%async_computation.5 | async-start | bytes 3145728 | tf_op jit(solution)/shard_map/all_to_all | solution.py:90
  448.4 44.6 %all-to-all-start.6 = ((f32[2,32,12,512]{3,0,2,1:T(2,128)}), f32[2,32,12,512]{3,0,2,1:T(2,128)}, u32[]{:S(2)}, u32[]{:S(2)}) async-start(f32[2,32,12,512]{3,0,2,1:T(2,128)} %copy.92), calls=%async_computation.6 | async-start | bytes 3145728 | tf_op jit(solution)/shard_map/all_to_all | solution.py:91
  456.2 75.4 %all-gather.2.cloned.1.call-start = ((), (), s32[]{:S(2)}) async-start(), calls=%async_computation.7 | async-start | bytes 3538944 | tf_op jit(solution)/shard_map/all_gather | solution.py:117
  464.0 34.0 %copy-start.2 = (f32[3,384,512]{2,1,0:T(8,128)S(1)}, f32[3,384,512]{2,1,0:T(8,128)}, u32[]{:S(2)}) copy-start(f32[3,384,512]{2,1,0:T(8,128)} %copy-done.1) | copy-start | bytes 7077892
  464.0 34.0 %copy-start.6 = (f32[512]{0:T(512)S(1)}, f32[512]{0:T(512)}, u32[]{:S(2)}) copy-start(f32[512]{0:T(512)} %param.12) | copy-start | bytes 6148
Sparse Core Ops, SparseCore 0:
  500.8 30.8 all-gather.1
where the time goes:
time: 548 us; the launch traced here: 544 us
  waiting for transfers between devices  319 us (58%)
  matrix products  95.5 us (17%)
  starting transfers between devices  61.3 us (11%)
  local copies, waits for them, and re-layouts  41.5 us (8%)
  between operations  14 us (3%)
  other arithmetic  13.5 us (2%)
    all_to_all x2, waiting for transfers between devices, sequence_conv(): lax.all_to_all(sectioned[0], 'seq', split_axis=1, concat_axis=2, tiled=True)  95 us
    dot_general x16, matrix products, contract(): return jnp.einsum(pattern, first_op, second_op, precision=highest)  89.8 us
    all_to_all x2, waiting for transfers between devices, sequence_conv(): lax.all_to_all(sectioned[1], 'seq', split_axis=1, concat_axis=2, tiled=True)  88.2 us
    all_to_all x1, waiting for transfers between devices, sequence_conv(): lax.all_to_all(planes, 'seq', split_axis=2, concat_axis=1, tiled=True)  36.7 us
    all_to_all x1, waiting for transfers between devices, sequence_conv(): lax.all_to_all(sectioned[0], 'seq', split_axis=2, concat_axis=1, tiled=True)  34.6 us
    all_to_all x1, waiting for transfers between devices, sequence_conv(): lax.all_to_all(sectioned[1], 'seq', split_axis=2, concat_axis=1, tiled=True)  33.1 us
    all_gather x1, waiting for transfers between devices, on_device(): lax.all_gather(mixed, 'ch', axis=1, tiled=True)  31 us
    all_to_all x2, starting transfers between devices, sequence_conv(): lax.all_to_all(sectioned[1], 'seq', split_axis=1, concat_axis=2, tiled=True)  15.6 us
  transfers between devices with their start and end apart: 9, of which 8 were waited for; matrix products, arithmetic and copies ran while one was open for 8% of the time, Pallas kernels for 0%

commit v1 on v0

--- a/solution.py
+++ b/solution.py
@@ -114,7 +114,9 @@
     filtered = long_out + skip_gain * mixed_in
     mixed = (gate_late * filtered).astype(jnp.bfloat16)
     summed = jnp.dot(
-        lax.all_gather(mixed, "ch", axis=1, tiled=True),
+        jnp.concatenate(
+            lax.all_to_all(jnp.stack([mixed] * lax.axis_size("ch")), "ch", 0, 0), axis=1
+        ),
         out_weight,
         preferred_element_type=jnp.float32,
     )

time: 548 us -> 544 us (level)
  blocking collectives: 0 us -> 46 us
  waiting for transfers between devices: 319 us -> 292 us
  between operations: 14 us -> 0.7 us
    all_to_all x0 -> x1, blocking collectives: none -> 46 us  [on_device(): lax.all_to_all(jnp.stack([mixed] * lax.axis_size('ch')), 'ch', 0, 0)]
    all_gather x1 -> x0, waiting for transfers between devices: 31 us -> none  [on_device(): lax.all_gather(mixed, 'ch', axis=1, tiled=True)]
  transfers between devices with their start and end apart: 9 -> 8, of which waited for: 8 -> 7; matrix products, arithmetic and copies ran while one was open for 8% -> 7% of each run, Pallas kernels for 0% -> 0%
where the time goes in v1:
time: 544 us; the launch traced here: 540 us
  waiting for transfers between devices  292 us (54%)
  matrix products  91.9 us (17%)
  starting transfers between devices  61.3 us (11%)
  blocking collectives  46 us (8%)
  local copies, waits for them, and re-layouts  37 us (7%)
  other arithmetic  10.8 us (2%)
    all_to_all x2, waiting for transfers between devices, sequence_conv(): lax.all_to_all(sectioned[0], 'seq', split_axis=1, concat_axis=2, tiled=True)  95 us
    all_to_all x2, waiting for transfers between devices, sequence_conv(): lax.all_to_all(sectioned[1], 'seq', split_axis=1, concat_axis=2, tiled=True)  92.5 us
    dot_general x16, matrix products, contract(): return jnp.einsum(pattern, first_op, second_op, precision=highest)  89.3 us
    all_to_all x1, blocking collectives, on_device(): lax.all_to_all(jnp.stack([mixed] * lax.axis_size('ch')), 'ch', 0, 0)  46 us
    all_to_all x1, waiting for transfers between devices, sequence_conv(): lax.all_to_all(planes, 'seq', split_axis=2, concat_axis=1, tiled=True)  36.7 us
    all_to_all x1, waiting for transfers between devices, sequence_conv(): lax.all_to_all(sectioned[0], 'seq', split_axis=2, concat_axis=1, tiled=True)  34.7 us
    all_to_all x1, waiting for transfers between devices, sequence_conv(): lax.all_to_all(sectioned[1], 'seq', split_axis=2, concat_axis=1, tiled=True)  33.1 us
    all_to_all x2, starting transfers between devices, sequence_conv(): lax.all_to_all(sectioned[1], 'seq', split_axis=1, concat_axis=2, tiled=True)  15.8 us
  transfers between devices with their start and end apart: 8, of which 7 were waited for; matrix products, arithmetic and copies ran while one was open for 7% of the time, Pallas kernels for 0%

profile of v1, /device:TPU:1, one launch (start us, length us, event | category | flops | bytes accessed | tf_op | source)
XLA Modules:
  0.0 539.7 jit_solution(7541904072780819813)
XLA Ops:
  12.6 12.3 %all-to-all-start = ((f32[2,1,384,512]{3,0,1,2:T(2,128)}), f32[2,1,384,512]{3,0,1,2:T(2,128)S(1)}, u32[]{:S(2)}, u32[]{:S(2)}) async-start(f32[2,1,384,512]{3,0,1,2:T(2,128)} %copy.102), calls=%async_computation | async-start | bytes 3145728 | tf_op jit(solution)/shard_map/all_to_all | solution.py:55
  25.1 36.7 %all-to-all-done = f32[2,1,384,512]{3,0,1,2:T(2,128)S(1)} async-done(((f32[2,1,384,512]{3,0,1,2:T(2,128)}), f32[2,1,384,512]{3,0,1,2:T(2,128)S(1)}, u32[]{:S(2)}, u32[]{:S(2)}) %all-to-all-start) | async-done | bytes 1572896 | tf_op jit(solution)/shard_map/all_to_all | solution.py:55
  73.9 5.6 %fusion = (f32[4,32,12,512]{3,1,2,0:T(8,128)S(1)}, f32[4,32,12,512]{3,1,2,0:T(8,128)}) fusion(f32[4,12,512,32]{2,3,1,0:T(8,128)S(1)} %convolution_subtract_fusion, f32[32,12]{0,1:T(8,128)S(1)} %get-tuple-element.27, f32[32,12]{0,1:T(8,128)S(1)} %get-tuple-element.26, f32[4,12,512,32]{2,3,1,0:T(8,128)S(1)} %fusion.2, ...), kind=kOutput, calls=%fused_computation.4 | convolution fusion | flops 309868544 | bytes 15731712 | tf_op jit(solution)/shard_map/kp,xpbc->xkbc/dot_general | solution.py:23
  83.3 7.3 %all-to-all-start.1 = ((f32[4,32,12,512]{3,0,2,1:T(4,128)}), f32[4,32,12,512]{3,0,2,1:T(4,128)S(1)}, u32[]{:S(2)}, u32[]{:S(2)}) async-start(f32[4,32,12,512]{3,0,2,1:T(4,128)} %copy.113), calls=%async_computation.1 | async-start | bytes 6291456 | tf_op jit(solution)/shard_map/all_to_all | solution.py:74
  90.6 5.5 %copy.115 = f32[4,32,12,512]{3,0,2,1:T(4,128)} copy(f32[4,32,12,512]{3,1,2,0:T(8,128)} %get-tuple-element.6) | data formatting | bytes 6291456 | tf_op jit(solution)/shard_map/add | solution.py:38
  96.1 65.8 %all-to-all-done.1 = f32[4,32,12,512]{3,0,2,1:T(4,128)S(1)} async-done(((f32[4,32,12,512]{3,0,2,1:T(4,128)}), f32[4,32,12,512]{3,0,2,1:T(4,128)S(1)}, u32[]{:S(2)}, u32[]{:S(2)}) %all-to-all-start.1) | async-done | bytes 3145760 | tf_op jit(solution)/shard_map/all_to_all | solution.py:74
  163.6 8.1 %all-to-all-start.2 = ((f32[4,32,12,512]{3,0,2,1:T(4,128)}), f32[4,32,12,512]{3,0,2,1:T(4,128)}, u32[]{:S(2)}, u32[]{:S(2)}) async-start(f32[4,32,12,512]{3,0,2,1:T(4,128)} %copy.115), calls=%async_computation.2 | async-start | bytes 6291456 | tf_op jit(solution)/shard_map/all_to_all | solution.py:75
  175.0 9.8 %fusion.43 = f32[4,512,384]{2,1,0:T(8,128)} fusion(f32[4,384,512]{1,2,0:T(8,128)S(1)} %copy.114), kind=kOutput, calls=%fused_computation.73 | convolution fusion | flops 3625205760 | bytes 6291456 | tf_op jit(solution)/shard_map/mb,xkbc->xkmc/dot_general | solution.py:23
  184.8 60.3 %all-to-all-done.2 = f32[4,32,12,512]{3,0,2,1:T(4,128)} async-done(((f32[4,32,12,512]{3,0,2,1:T(4,128)}), f32[4,32,12,512]{3,0,2,1:T(4,128)}, u32[]{:S(2)}, u32[]{:S(2)}) %all-to-all-start.2) | async-done | bytes 3145760 | tf_op jit(solution)/shard_map/all_to_all | solution.py:75
  250.2 10.7 %fusion.41 = f32[4,512,384]{2,1,0:T(8,128)S(1)} fusion(f32[4,384,512]{1,2,0:T(8,128)} %copy.116), kind=kOutput, calls=%fused_computation.71 | convolution fusion | flops 3625205760 | bytes 6291456 | tf_op jit(solution)/shard_map/mb,xkbc->xkmc/dot_general | solution.py:23
  260.9 9.0 %subtract_bitcast_fusion = f32[4,1,384,512]{2,3,0,1:T(8,128)S(1)} fusion(f32[4,512,384]{2,1,0:T(8,128)S(1)} %copy-done.4, f32[4,384,512]{1,2,0:T(8,128)S(1)} %copy-done), kind=kOutput, calls=%fused_computation.9 | convolution fusion | flops 3625992192 | bytes 9437184 | tf_op jit(solution)/shard_map/mb,xkbc->xkmc/dot_general | solution.py:23
  269.9 9.2 %add_bitcast_fusion = f32[4,1,384,512]{2,3,0,1:T(8,128)S(1)} fusion(f32[4,512,384]{2,1,0:T(8,128)S(1)} %fusion.41, f32[4,384,512]{1,2,0:T(8,128)S(1)} %copy.114), kind=kOutput, calls=%fused_computation.8 | convolution fusion | flops 3625992192 | bytes 9437184 | tf_op jit(solution)/shard_map/mb,xkbc->xkmc/dot_general | solution.py:23
  284.9 5.6 %fusion.10 = f32[2,512,384]{2,1,0:T(8,128)S(1)} fusion(f32[2,1,384,512]{2,3,0,1:T(8,128)S(1)} %get-tuple-element.8), kind=kOutput, calls=%fused_computation.28 | convolution fusion | flops 1813266432 | bytes 3145728 | tf_op jit(solution)/shard_map/mb,xkmc->xkbc/dot_general | solution.py:23
  290.5 5.4 %fusion.18 = f32[2,512,384]{2,1,0:T(8,128)S(1)} fusion(f32[2,512,384]{2,1,0:T(8,128)S(1)} %fusion.12, f32[2,1,384,512]{2,3,0,1:T(8,128)S(1)} %get-tuple-element.7), kind=kOutput, calls=%fused_computation.40 | convolution fusion | flops 1813659648 | bytes 4718592 | tf_op jit(solution)/shard_map/mb,xkmc->xkbc/dot_general | solution.py:23
  295.9 5.5 %fusion.7 = (f32[2,1,384,512]{2,3,0,1:T(8,128)S(1)}, f32[2,1,384,512]{2,3,0,1:T(8,128)S(1)}) fusion(f32[2,512,384]{2,1,0:T(8,128)S(1)} %fusion.18, f32[384]{0:T(512)S(1)} %get-tuple-element.32, f32[384]{0:T(512)S(1)} %get-tuple-element.33, f32[2,512,384]{2,1,0:T(8,128)S(1)} %fusion.10, f32[2,1,384,512]{2,3,0,1:T(8,128)S(1)} %get-tuple-element.7), kind=kOutput, calls=%fused_computation.23 | convolution fusion | flops 1816018944 | bytes 7867392 | tf_op jit(solution)/shard_map/mb,xkmc->xkbc/dot_general | solution.py:23
  303.5 5.8 %all-to-all-start.3 = ((f32[2,1,384,512]{3,0,1,2:T(2,128)}), f32[2,1,384,512]{3,0,1,2:T(2,128)S(1)}, u32[]{:S(2)}, u32[]{:S(2)}) async-start(f32[2,1,384,512]{3,0,1,2:T(2,128)} %copy.119), calls=%async_computation.3 | async-start | bytes 3145728 | tf_op jit(solution)/shard_map/all_to_all | solution.py:83
  311.3 34.7 %all-to-all-done.3 = f32[2,1,384,512]{3,0,1,2:T(2,128)S(1)} async-done(((f32[2,1,384,512]{3,0,1,2:T(2,128)}), f32[2,1,384,512]{3,0,1,2:T(2,128)S(1)}, u32[]{:S(2)}, u32[]{:S(2)}) %all-to-all-start.3) | async-done | bytes 1572896 | tf_op jit(solution)/shard_map/all_to_all | solution.py:83
  346.0 7.7 %all-to-all-start.4 = ((f32[2,1,384,512]{3,0,1,2:T(2,128)}), f32[2,1,384,512]{3,0,1,2:T(2,128)S(1)}, u32[]{:S(2)}, u32[]{:S(2)}) async-start(f32[2,1,384,512]{3,0,1,2:T(2,128)} %copy.121), calls=%async_computation.4 | async-start | bytes 3145728 | tf_op jit(solution)/shard_map/all_to_all | solution.py:84
  357.4 33.1 %all-to-all-done.4 = f32[2,1,384,512]{3,0,1,2:T(2,128)S(1)} async-done(((f32[2,1,384,512]{3,0,1,2:T(2,128)}), f32[2,1,384,512]{3,0,1,2:T(2,128)S(1)}, u32[]{:S(2)}, u32[]{:S(2)}) %all-to-all-start.4) | async-done | bytes 1572896 | tf_op jit(solution)/shard_map/all_to_all | solution.py:84
  396.9 8.0 %all-to-all-start.5 = ((f32[2,32,12,512]{3,0,2,1:T(2,128)}), f32[2,32,12,512]{3,0,2,1:T(2,128)}, u32[]{:S(2)}, u32[]{:S(2)}) async-start(f32[2,32,12,512]{3,0,2,1:T(2,128)} %copy.123), calls=%async_computation.5 | async-start | bytes 3145728 | tf_op jit(solution)/shard_map/all_to_all | solution.py:90
  412.5 29.2 %all-to-all-done.5 = f32[2,32,12,512]{3,0,2,1:T(2,128)} async-done(((f32[2,32,12,512]{3,0,2,1:T(2,128)}), f32[2,32,12,512]{3,0,2,1:T(2,128)}, u32[]{:S(2)}, u32[]{:S(2)}) %all-to-all-start.5) | async-done | bytes 1572896 | tf_op jit(solution)/shard_map/all_to_all | solution.py:90
  441.7 7.8 %all-to-all-start.6 = ((f32[2,32,12,512]{3,0,2,1:T(2,128)}), f32[2,32,12,512]{3,0,2,1:T(2,128)}, u32[]{:S(2)}, u32[]{:S(2)}) async-start(f32[2,32,12,512]{3,0,2,1:T(2,128)} %copy.128), calls=%async_computation.6 | async-start | bytes 3145728 | tf_op jit(solution)/shard_map/all_to_all | solution.py:91
  454.0 32.3 %all-to-all-done.6 = f32[2,32,12,512]{3,0,2,1:T(2,128)} async-done(((f32[2,32,12,512]{3,0,2,1:T(2,128)}), f32[2,32,12,512]{3,0,2,1:T(2,128)}, u32[]{:S(2)}, u32[]{:S(2)}) %all-to-all-start.6) | async-done | bytes 1572896 | tf_op jit(solution)/shard_map/all_to_all | solution.py:91
  490.8 46.0 %all_to_all.74 = bf16[8,384,512]{1,2,0:T(8,128)(2,1)S(1)} all-to-all(bf16[8,384,512]{1,2,0:T(8,128)(2,1)S(1)} %stack.51), channel_id=1, replica_groups=mesh['seq'=32,'ch'=8] {'ch'}, dimensions={0} | all-to-all | bytes 6291456 | tf_op jit(solution)/shard_map/all_to_all | solution.py:118
  (59 shorter events, 77.7 us)
Async XLA Ops:
  0.7 5.3 collective-permute-start
  8.3 1.8 copy-start.1
  8.3 1.7 copy-start.5
  12.6 49.2 %all-to-all-start = ((f32[2,1,384,512]{3,0,1,2:T(2,128)}), f32[2,1,384,512]{3,0,1,2:T(2,128)S(1)}, u32[]{:S(2)}, u32[]{:S(2)}) async-start(f32[2,1,384,512]{3,0,1,2:T(2,128)} %copy.102), calls=%async_computation | async-start | bytes 3145728 | tf_op jit(solution)/shard_map/all_to_all | solution.py:55
  83.3 78.6 %all-to-all-start.1 = ((f32[4,32,12,512]{3,0,2,1:T(4,128)}), f32[4,32,12,512]{3,0,2,1:T(4,128)S(1)}, u32[]{:S(2)}, u32[]{:S(2)}) async-start(f32[4,32,12,512]{3,0,2,1:T(4,128)} %copy.113), calls=%async_computation.1 | async-start | bytes 6291456 | tf_op jit(solution)/shard_map/all_to_all | solution.py:74
  161.9 1.7 copy-start.3
  163.6 81.4 %all-to-all-start.2 = ((f32[4,32,12,512]{3,0,2,1:T(4,128)}), f32[4,32,12,512]{3,0,2,1:T(4,128)}, u32[]{:S(2)}, u32[]{:S(2)}) async-start(f32[4,32,12,512]{3,0,2,1:T(4,128)} %copy.115), calls=%async_computation.2 | async-start | bytes 6291456 | tf_op jit(solution)/shard_map/all_to_all | solution.py:75
  250.2 10.7 %copy-start = (f32[4,384,512]{1,2,0:T(8,128)S(1)}, f32[4,384,512]{1,2,0:T(8,128)}, u32[]{:S(2)}) copy-start(f32[4,384,512]{1,2,0:T(8,128)} %copy.116) | copy-start | bytes 9437188
  250.2 10.7 %copy-start.4 = (f32[4,512,384]{2,1,0:T(8,128)S(1)}, f32[4,512,384]{2,1,0:T(8,128)}, u32[]{:S(2)}) copy-start(f32[4,512,384]{2,1,0:T(8,128)} %fusion.43) | copy-start | bytes 9437188
  303.5 42.5 %all-to-all-start.3 = ((f32[2,1,384,512]{3,0,1,2:T(2,128)}), f32[2,1,384,512]{3,0,1,2:T(2,128)S(1)}, u32[]{:S(2)}, u32[]{:S(2)}) async-start(f32[2,1,384,512]{3,0,1,2:T(2,128)} %copy.119), calls=%async_computation.3 | async-start | bytes 3145728 | tf_op jit(solution)/shard_map/all_to_all | solution.py:83
  346.0 44.5 %all-to-all-start.4 = ((f32[2,1,384,512]{3,0,1,2:T(2,128)}), f32[2,1,384,512]{3,0,1,2:T(2,128)S(1)}, u32[]{:S(2)}, u32[]{:S(2)}) async-start(f32[2,1,384,512]{3,0,1,2:T(2,128)} %copy.121), calls=%async_computation.4 | async-start | bytes 3145728 | tf_op jit(solution)/shard_map/all_to_all | solution.py:84
  396.9 44.8 %all-to-all-start.5 = ((f32[2,32,12,512]{3,0,2,1:T(2,128)}), f32[2,32,12,512]{3,0,2,1:T(2,128)}, u32[]{:S(2)}, u32[]{:S(2)}) async-start(f32[2,32,12,512]{3,0,2,1:T(2,128)} %copy.123), calls=%async_computation.5 | async-start | bytes 3145728 | tf_op jit(solution)/shard_map/all_to_all | solution.py:90
  441.7 44.6 %all-to-all-start.6 = ((f32[2,32,12,512]{3,0,2,1:T(2,128)}), f32[2,32,12,512]{3,0,2,1:T(2,128)}, u32[]{:S(2)}, u32[]{:S(2)}) async-start(f32[2,32,12,512]{3,0,2,1:T(2,128)} %copy.128), calls=%async_computation.6 | async-start | bytes 3145728 | tf_op jit(solution)/shard_map/all_to_all | solution.py:91
  451.8 37.0 %copy-start.2 = (f32[3,384,512]{2,1,0:T(8,128)S(1)}, f32[3,384,512]{2,1,0:T(8,128)}, u32[]{:S(2)}) copy-start(f32[3,384,512]{2,1,0:T(8,128)} %copy-done.1) | copy-start | bytes 7077892
  451.9 37.0 %copy-start.6 = (f32[512]{0:T(512)S(1)}, f32[512]{0:T(512)}, u32[]{:S(2)}) copy-start(f32[512]{0:T(512)} %param.12) | copy-start | bytes 6148
  490.8 46.0 %copy-start.7 = (bf16[4096,512]{1,0:T(8,128)(2,1)S(1)}, bf16[4096,512]{1,0:T(8,128)(2,1)}, u32[]{:S(2)}) copy-start(bf16[4096,512]{1,0:T(8,128)(2,1)} %param.13) | copy-start | bytes 12582916
